TPU v7x, 128 devices: a whole 4x4x4 slice. The times are simulated.
128 devices in a mesh: ctx: 32 (over y, x, core), tp: 4 (over z).
Axes of the slice: x: 4, y: 4, z: 4, core: 2. Of those that a mesh axis runs over, the one named last changes fastest.
Arguments:
- hidden: bfloat16 [8192, 5120], P('ctx', 'tp'), may hold values from -6 to 6
- queries: bfloat16 [8192, 5120], P('ctx', 'tp'), may hold values from -28 to 28
- key_weight: bfloat16 [5120, 1024], P(None, 'tp'), may hold values from -0.078125 to 0.078125
- value_weight: bfloat16 [5120, 1024], P(None, 'tp'), may hold values from -0.078125 to 0.078125
- parents: int32 [64], replicated, may hold values from -1 to 62, as said below
- upstream: bfloat16 [8192, 5120], P('ctx', 'tp'), may hold values from -6 to 6
Outputs:
- attention: bfloat16 [8192, 5120], P('ctx', 'tp')
- query_grad: bfloat16 [8192, 5120], P('ctx', 'tp')
- hidden_grad: bfloat16 [8192, 5120], P('ctx', 'tp')
- key_weight_grad: float32 [5120, 1024], P('ctx', 'tp')
- value_weight_grad: float32 [5120, 1024], P('ctx', 'tp')
Inputs may be any that keep to these rules, and one draw needn't show every extreme that they name: Node blocks lie in depth-first order: parents[b] < b is the parent of block b for b > 0, parents[0] = -1 and block 0 is the only root; no root-to-leaf path holds more than 8 blocks; the last 7 blocks form one chain below block 0, so that the last block's path holds exactly 8 blocks.
All inputs are finite; a program needn't handle non-finite values.
Results may differ from a plain program's by a relative error of at most 0.023.
The roundings to bfloat16 on the way count: a program that leaves them out, or rounds other values in their place, can miss the bound.
Values may be sent and summed in bfloat16 or wider, within the bound.
No kernel may reach another device: no remote copies, remote signals or barrier semaphores. Data moves between devices by JAX's collectives and lax.ppermute only.
A program may use at most 128 MiB of HBM per device.

v0:
```python
from functools import partial
import math
import jax
import jax.numpy as jnp
from jax import lax
from jax.sharding import PartitionSpec as P

HD = 128
BLOCK = 128
DEPTH = 8
THETA = 1000000.0
NEGATIVE = -1e30
HIGHEST = lax.Precision.HIGHEST


def tree_tables(parents, block_total, depth_slots):
    indices = jnp.arange(block_total, dtype=jnp.int32)
    parent_link = (parents[:, None] == indices[None, :]).astype(jnp.float32)
    closure = jnp.eye(block_total, dtype=jnp.float32) + parent_link
    for repeat in range(depth_slots.bit_length()):
        closure = jnp.minimum(
            jnp.dot(closure, closure, precision=HIGHEST, preferred_element_type=jnp.float32), 1.0
        )
    closure_int = closure.astype(jnp.int32)
    depths = jnp.sum(closure_int, axis=1) - 1
    levels = jnp.arange(depth_slots, dtype=jnp.int32)
    select = closure_int[:, :, None] * (depths[None, :, None] == levels[None, None, :]).astype(
        jnp.int32
    )
    path_ids = jnp.sum(select * indices[None, :, None], axis=1) + jnp.sum(select, axis=1) - 1
    return (depths, path_ids)


def rope_angles(depths, block_len, head_width):
    offset = jnp.arange(block_len, dtype=jnp.int32)
    position = (depths[:, None] * block_len + offset[None, :]).astype(jnp.float32)
    midpoint = head_width // 2
    frequency = jnp.exp(
        jnp.arange(midpoint, dtype=jnp.float32) * (-2.0 * math.log(THETA) / head_width)
    )
    angles = position[:, :, None] * frequency[None, None, :]
    return (jnp.cos(angles), jnp.sin(angles))


def rotate_pairs(fields, cosine, sine_table, direction):
    midpoint = fields.shape[-1] // 2
    leading = fields[..., :midpoint]
    trailing = fields[..., midpoint:]
    cos_part = cosine[:, :, None, :]
    sin_part = direction * sine_table[:, :, None, :]
    return jnp.concatenate(
        [leading * cos_part - trailing * sin_part, trailing * cos_part + leading * sin_part],
        axis=-1,
    )


def allowed_mask(depths, block_len, slot_count):
    query_pos = jnp.arange(block_len, dtype=jnp.int32)
    key_index = jnp.arange(slot_count * block_len, dtype=jnp.int32)
    key_slot = key_index // block_len
    key_offset = key_index % block_len
    earlier = key_slot[None, None, :] < depths[:, None, None]
    itself = (key_slot[None, None, :] == depths[:, None, None]) & (
        key_offset[None, None, :] <= query_pos[None, :, None]
    )
    return earlier | itself


def attend_block(query_blocks, key_rows, value_rows, allowed, upstream_blocks, score_scale):
    scores = (
        jnp.einsum("bqhgd,bkhd->bhgqk", query_blocks, key_rows, preferred_element_type=jnp.float32)
        * score_scale
    )
    scores = jnp.where(allowed[:, None, None], scores, NEGATIVE)
    maximum = jnp.max(scores, axis=-1, keepdims=True)
    weights = jnp.exp(scores - maximum)
    totals = jnp.sum(weights, axis=-1, keepdims=True)
    mixed_rows = jnp.einsum(
        "bhgqk,bkhd->bqhgd",
        weights.astype(jnp.bfloat16),
        value_rows,
        preferred_element_type=jnp.float32,
    )
    totals_rows = jnp.transpose(totals, (0, 3, 1, 2, 4))
    output = (mixed_rows / totals_rows).astype(jnp.bfloat16)
    logsum = maximum + jnp.log(totals)
    deltas = jnp.sum(upstream_blocks.astype(jnp.float32) * output.astype(jnp.float32), axis=-1)
    deltas = jnp.transpose(deltas, (0, 2, 3, 1))[..., None]
    probabilities = jnp.exp(scores - logsum)
    value_grad = jnp.einsum(
        "bhgqk,bqhgd->bkhd",
        probabilities.astype(jnp.bfloat16),
        upstream_blocks,
        preferred_element_type=jnp.float32,
    )
    prob_grad = jnp.einsum(
        "bqhgd,bkhd->bhgqk", upstream_blocks, value_rows, preferred_element_type=jnp.float32
    )
    score_grad = (probabilities * (prob_grad - deltas)).astype(jnp.bfloat16)
    query_grad = (
        jnp.einsum("bhgqk,bkhd->bqhgd", score_grad, key_rows, preferred_element_type=jnp.float32)
        * score_scale
    ).astype(jnp.bfloat16)
    key_grad = (
        jnp.einsum(
            "bhgqk,bqhgd->bkhd", score_grad, query_blocks, preferred_element_type=jnp.float32
        )
        * score_scale
    )
    return (output, query_grad, key_grad, value_grad)


def shards(hidden, queries, key_weight, value_weight, parents, upstream):
    local_rows = hidden.shape[0]
    blocks = local_rows // BLOCK
    block_total = parents.shape[0]
    key_width = key_weight.shape[1]
    key_heads = key_width // HD
    groups = queries.shape[1] // key_width
    pair_width = 2 * key_width
    score_scale = 1.0 / math.sqrt(HD)
    first_block = lax.axis_index("ctx") * blocks
    depth_all, path_all = tree_tables(parents, block_total, DEPTH)
    depths = lax.dynamic_slice_in_dim(depth_all, first_block, blocks, 0)
    path_ids = lax.dynamic_slice_in_dim(path_all, first_block, blocks, 0)
    cosine, sine_table = rope_angles(depths, BLOCK, HD)
    features = lax.all_gather(hidden, "tp", axis=1, tiled=True)
    key_linear = jnp.dot(features, key_weight, preferred_element_type=jnp.float32).reshape(
        blocks, BLOCK, key_heads, HD
    )
    key_rotated = (
        rotate_pairs(key_linear, cosine, sine_table, 1.0)
        .astype(jnp.bfloat16)
        .reshape(local_rows, key_width)
    )
    value_rows = jnp.dot(features, value_weight, preferred_element_type=jnp.float32).astype(
        jnp.bfloat16
    )
    key_value = jnp.concatenate([key_rotated, value_rows], axis=1)
    gathered = lax.all_gather(key_value, "ctx", axis=0, tiled=True).reshape(
        block_total, BLOCK, pair_width
    )
    slot_rows = gathered[jnp.clip(path_ids, 0, block_total - 1)]
    query_blocks = queries.reshape(blocks, BLOCK, key_heads, groups, HD)
    upstream_blocks = upstream.reshape(blocks, BLOCK, key_heads, groups, HD)

    def attend_slots(slot_count):
        chosen = slot_rows[:, :slot_count].reshape(blocks, slot_count * BLOCK, pair_width)
        key_part = chosen[..., :key_width].reshape(blocks, slot_count * BLOCK, key_heads, HD)
        value_part = chosen[..., key_width:].reshape(blocks, slot_count * BLOCK, key_heads, HD)
        allowed = allowed_mask(depths, BLOCK, slot_count)
        output, query_grad, key_grad, value_grad = attend_block(
            query_blocks, key_part, value_part, allowed, upstream_blocks, score_scale
        )
        slot_grads = jnp.concatenate(
            [
                key_grad.reshape(blocks, slot_count, BLOCK, key_width),
                value_grad.reshape(blocks, slot_count, BLOCK, key_width),
            ],
            axis=-1,
        )
        slot_grads = jnp.pad(slot_grads, ((0, 0), (0, DEPTH - slot_count), (0, 0), (0, 0)))
        return (
            output.reshape(local_rows, groups * key_width),
            query_grad.reshape(local_rows, groups * key_width),
            slot_grads,
        )

    needed = jnp.max(depths) + 1
    bucket = (needed > DEPTH // 4).astype(jnp.int32) + (needed > DEPTH // 2).astype(jnp.int32)
    bucket_sizes = [DEPTH // 4, DEPTH // 2, DEPTH]
    attention, query_grad, slot_grads = lax.switch(
        bucket, [partial(attend_slots, slot_count) for slot_count in bucket_sizes]
    )
    flat_grads = slot_grads.reshape(blocks * DEPTH, BLOCK * pair_width)
    block_targets = path_ids.reshape(blocks * DEPTH)
    block_count = local_rows * lax.axis_size("ctx") // BLOCK
    selector = (block_targets[None, :] == jnp.arange(block_count, dtype=jnp.int32)[:, None]).astype(
        jnp.float32
    )
    pair_grads = lax.psum_scatter(
        jnp.dot(
            selector, flat_grads, precision=HIGHEST, preferred_element_type=jnp.float32
        ).reshape(local_rows * lax.axis_size("ctx"), pair_width),
        "ctx",
        scatter_dimension=0,
        tiled=True,
    )
    key_total = pair_grads[:, :key_width].reshape(blocks, BLOCK, key_heads, HD)
    key_linear_grad = (
        rotate_pairs(key_total, cosine, sine_table, -1.0)
        .astype(jnp.bfloat16)
        .reshape(local_rows, key_width)
    )
    value_grad_rows = pair_grads[:, key_width:].astype(jnp.bfloat16)
    grad_pairs = jnp.concatenate([key_linear_grad, value_grad_rows], axis=1)
    weight_grads = lax.psum_scatter(
        jnp.einsum("tc,tw->cw", features, grad_pairs, preferred_element_type=jnp.float32),
        "ctx",
        scatter_dimension=0,
        tiled=True,
    )
    partial_input = jnp.einsum(
        "tw,dw->td", key_linear_grad, key_weight, preferred_element_type=jnp.float32
    )
    partial_input = partial_input + jnp.einsum(
        "tw,dw->td", value_grad_rows, value_weight, preferred_element_type=jnp.float32
    )
    hidden_grad = lax.psum_scatter(
        partial_input.astype(jnp.bfloat16), "tp", scatter_dimension=1, tiled=True
    )
    return (
        attention,
        query_grad,
        hidden_grad,
        weight_grads[:, :key_width],
        weight_grads[:, key_width:],
    )


def solution(mesh):
    return jax.shard_map(
        shards,
        mesh=mesh,
        in_specs=(
            P("ctx", "tp"),
            P("ctx", "tp"),
            P(None, "tp"),
            P(None, "tp"),
            P(),
            P("ctx", "tp"),
        ),
        out_specs=(P("ctx", "tp"), P("ctx", "tp"), P("ctx", "tp"), P("ctx", "tp"), P("ctx", "tp")),
        check_vma=False,
    )
```

profile of v0, /device:TPU:1, one launch (start us, length us, event | category | flops | bytes accessed | tf_op | source)
XLA Modules:
  0.0 535.3 jit_solution(10421093804757671469)
XLA Ops:
  7.2 0.7 all-gather.3.cloned.1.call-update
  8.0 1.0 convolution_minimum_fusion.3
  9.0 0.2 convolution_minimum_fusion.2
  9.1 0.2 convolution_minimum_fusion.1
  9.3 0.9 fusion.127
  10.3 1.3 broadcast_multiply_fusion
  11.6 36.5 %all-gather.3.cloned.1.call-done = bf16[256,5120]{1,0:T(8,128)(2,1)} async-done(((bf16[256,1280]{1,0:T(8,128)(2,1)}), bf16[256,5120]{1,0:T(8,128)(2,1)}) %all-gather.3.cloned.1.call-update) | async-done | bytes 2621456 | tf_op jit(solution)/shard_map/all_gather | solution.py:127
  48.1 2.6 fusion.129
  50.7 0.1 reshape.522
  50.8 1.5 subtract_convert_fusion.1
  52.4 0.4 pad_maximum_fusion.2
  52.9 3.7 convolution_convert_fusion
  56.5 0.7 pad_maximum_fusion.1
  57.3 0.6 reduce_max.36
  58.6 3.0 fusion.108
  61.6 0.7 eq.104
  62.3 54.3 %all-gather.5.cloned.1.call-done = bf16[8192,512]{0,1:T(8,128)(2,1)} async-done(((bf16[256,512]{0,1:T(8,128)(2,1)}), bf16[8192,512]{0,1:T(8,128)(2,1)}) %all-gather.5.cloned.1.call-update) | async-done | bytes 8388624 | tf_op jit(solution)/shard_map/all_gather | solution.py:140
  116.6 96.7 %conditional.1 = (f32[16,65536]{1,0:T(8,128)}, bf16[256,1280]{1,0:T(8,128)(2,1)}, bf16[256,1280]{1,0:T(8,128)(2,1)}) conditional(s32[]{:T(128)} %clamp.4, (s32[2]{0:T(128)S(1)}, bf16[8192,512]{0,1:T(8,128)(2,1)}, s32[]{:T(128)}, bf16[256,1280]{1,0:T(8,128)(2,1)S(1)}, bf16[256,1280]{1,0:T(8,128)(2,1)}, ...), branch_computations={%region_4.8_spmd.clone, %region_8.12_spmd.clone, %region_12.16_spm... | conditional | flops 4086446080 | bytes 220787328 | solution.py:172
  123.4 0.1 iota_compare_fusion.3
  123.5 0.3 and_or_fusion.1
  123.9 1.7 reshape.603
  125.6 2.6 reshape.617
  128.1 2.4 copy.374
  130.5 12.0 %copy.377 = bf16[8192,512]{1,0:T(8,128)(2,1)} copy(bf16[8192,512]{0,1:T(8,128)(2,1)} %get-tuple-element.247) | data formatting | bytes 16777216 | tf_op jit(solution)/shard_map
  142.5 5.4 %gather_fusion.1 = bf16[16,128,512]{2,1,0:T(8,128)(2,1)} fusion(bf16[64,128,512]{2,1,0:T(8,128)(2,1)} %bitcast.314, s32[1024]{0:T(1024)S(1)} %pad_clamp_fusion.1), kind=kCustom, calls=%fused_computation.1.clone | custom fusion | bytes 4194368 | tf_op jit(solution)/shard_map/gather | solution.py:143
  147.9 1.3 slice.74
  149.2 0.9 fusion.124
  150.1 1.0 copy.397
  151.1 1.3 copy.396
  152.4 2.4 fusion.30
  154.8 1.1 fusion.26
  155.9 0.4 copy-done.19
  156.3 0.6 copy-done.21
  156.9 2.4 multiply_reduce_fusion.1
  159.3 2.6 copy.380
  161.9 2.7 reshape.604
  164.7 5.0 fusion.46
  169.7 4.3 fusion.25
  174.0 0.9 fusion.51
  174.9 1.9 fusion.52
  176.8 1.8 copy.375
  178.6 3.1 reshape.599
  181.7 3.1 copy.376
  184.8 3.1 reshape.600
  187.9 1.5 copy.381
  189.4 2.6 reshape.605
  191.9 2.1 fusion.29
  194.0 4.5 copy.407
  213.3 12.3 %fusion.115 = f32[64,65536]{1,0:T(8,128)} fusion(f32[16,65536]{1,0:T(8,128)} %get-tuple-element.101, s32[16]{0:T(128)} %eq.104), kind=kOutput, calls=%fused_computation.186 | convolution fusion | flops 805307392 | bytes 20971584 | tf_op jit(solution)/shard_map/dot_general | solution.py:182
  225.5 14.5 %reshape.523 = f32[8192,512]{1,0:T(8,128)} reshape(f32[64,65536]{1,0:T(8,128)} %fusion.115) | data formatting | bytes 33554432 | tf_op jit(solution)/shard_map/reshape | solution.py:184
  240.1 131.5 %reduce-scatter.6.cloned.1.call-done = f32[256,512]{1,0:T(8,128)} async-done(((f32[8192,512]{1,0:T(8,128)}), f32[256,512]{1,0:T(8,128)}) %reduce-scatter.6.cloned.1.call-update) | async-done | bytes 524304 | tf_op jit(solution)/shard_map/reduce_scatter | solution.py:181
  371.6 1.0 slice.81
  372.6 0.1 reshape.524
  372.8 0.5 subtract_convert_fusion
  373.3 0.4 pad_maximum_fusion.3
  373.7 1.0 slice.96
  374.6 7.1 %convolution_bitcast_fusion.3 = f32[5120,512]{0,1:T(8,128)} fusion(bf16[256,5120]{1,0:T(8,128)(2,1)} %all-gather.3.cloned.1.call-done, bf16[256,256]{1,0:T(8,128)(2,1)S(1)} %slice.96, bf16[256,256]{1,0:T(8,128)(2,1)S(1)} %bitcast.337), kind=kOutput, calls=%fused_computation.152 | convolution fusion | flops 1342701568 | bytes 13369344 | tf_op jit(solution)/shard_map/tc,tw->cw/dot_general | solution.py:198
  381.8 11.4 %copy.336 = f32[5120,512]{1,0:T(8,128)} copy(f32[5120,512]{0,1:T(8,128)} %convolution_bitcast_fusion.3) | data formatting | bytes 20971520
  393.2 0.9 fusion.121
  394.2 0.9 copy-done.5
  395.1 2.5 fusion.106
  397.6 92.8 %reduce-scatter.10.cloned.1.call-done = f32[160,512]{1,0:T(8,128)} async-done(((f32[5120,512]{1,0:T(8,128)}), f32[160,512]{1,0:T(8,128)}) %reduce-scatter.10.cloned.1.call-update) | async-done | bytes 327696
  490.4 1.7 fusion.126
  492.1 36.4 %reduce-scatter.8.cloned.1.call-done = bf16[256,1280]{1,0:T(8,128)(2,1)} async-done(((bf16[256,5120]{1,0:T(8,128)(2,1)}), bf16[256,1280]{1,0:T(8,128)(2,1)}) %reduce-scatter.8.cloned.1.call-update) | async-done | bytes 655376 | tf_op jit(solution)/shard_map/reduce_scatter | solution.py:209
  (48 shorter events, 0.9 us)
Async XLA Ops:
  7.2 40.9 %copy-start = (bf16[5120,256]{1,0:T(8,128)(2,1)S(1)}, bf16[5120,256]{1,0:T(8,128)(2,1)}, u32[]{:S(2)}) copy-start(bf16[5120,256]{1,0:T(8,128)(2,1)} %param.11) | copy-start | bytes 7864324
  7.2 40.9 %all-gather.3.cloned.1.call-start = ((), (), s32[]{:S(2)}) async-start(), calls=%async_computation.3 | async-start | bytes 3276800 | tf_op jit(solution)/shard_map/all_gather | solution.py:127
  7.9 108.7 %all-gather.5.cloned.1.call-start = ((), (), s32[]{:S(2)}) async-start(), calls=%async_computation.4 | async-start | bytes 8650752 | tf_op jit(solution)/shard_map/all_gather | solution.py:140
  50.8 65.8 %copy-start.8 = (bf16[256,1280]{1,0:T(8,128)(2,1)S(1)}, bf16[256,1280]{1,0:T(8,128)(2,1)}, u32[]{:S(2)}) copy-start(bf16[256,1280]{1,0:T(8,128)(2,1)} %param.10) | copy-start | bytes 1966084
  57.3 314.4 %reduce-scatter.6.cloned.1.call-start = ((), (), s32[]{:S(2)}) async-start(), calls=%async_computation.5 | async-start | bytes 17301504 | tf_op jit(solution)/shard_map/reduce_scatter | solution.py:181
  154.8 4.6 copy-start.4
  154.8 1.6 copy-start.19
  154.8 2.1 copy-start.21
  164.7 5.0 copy-start.20
  164.7 5.0 copy-start.22
  169.7 4.3 copy-start.11
  176.8 11.1 %copy-start.12 = (bf16[2,128,2,5,128]{4,1,3,2,0:T(8,128)(2,1)S(1)}, bf16[2,128,2,5,128]{4,1,3,2,0:T(8,128)(2,1)}, u32[]{:S(2)}) copy-start(bf16[2,128,2,5,128]{4,1,3,2,0:T(8,128)(2,1)} %fusion.52) | copy-start | bytes 1966084 | tf_op jit(solution)/shard_map/cond
  240.1 132.7 %copy-start.14 = (f32[2,128,64]{2,1,0:T(8,128)S(1)}, f32[2,128,64]{2,1,0:T(8,128)}, u32[]{:S(2)}) copy-start(f32[2,128,64]{2,1,0:T(8,128)} %get-tuple-element.306) | copy-start | bytes 196612
  240.1 132.7 %copy-start.23 = (f32[2,128,64]{2,1,0:T(8,128)S(1)}, f32[2,128,64]{2,1,0:T(8,128)}, u32[]{:S(2)}) copy-start(f32[2,128,64]{2,1,0:T(8,128)} %get-tuple-element.304) | copy-start | bytes 196612
  240.1 250.3 %reduce-scatter.10.cloned.1.call-start = ((), (), s32[]{:S(2)}) async-start(), calls=%async_computation.7 | async-start | bytes 10813440
  393.2 1.0 copy-start.18
  393.2 135.4 %reduce-scatter.8.cloned.1.call-start = ((), (), s32[]{:S(2)}) async-start(), calls=%async_computation.6 | async-start | bytes 3276800 | tf_op jit(solution)/shard_map/reduce_scatter | solution.py:209
  393.2 1.9 copy-start.5
Sparse Core Ops, SparseCore 0:
  9.6 38.4 all-gather.2
  57.4 59.1 all-gather.4
  240.2 131.3 reduce-scatter.5
  393.3 97.0 reduce-scatter.9
  493.2 35.3 reduce-scatter.7
where the time goes:
time: 541 us; the launch traced here: 535 us
  waiting for transfers between devices  352 us (65%)
  local copies, waits for them, and re-layouts  86.2 us (16%)
  matrix products  48 us (9%)
  loops' own time  21.5 us (4%)
  between operations  14.9 us (3%)
  other arithmetic  12.3 us (2%)
    reduce_scatter x1, waiting for transfers between devices, shards(): lax.psum_scatter(jnp.dot(selector, flat_grads, precision=HIGHEST, preferr...  132 us
    unnamed x6, waiting for transfers between devices  93.5 us
    all_gather x1, waiting for transfers between devices, shards(): lax.all_gather(key_value, 'ctx', axis=0, tiled=True)  54.3 us
    all_gather x1, waiting for transfers between devices, shards(): features = lax.all_gather(hidden, 'tp', axis=1, tiled=True)  36.5 us
    reduce_scatter x1, waiting for transfers between devices, shards(): lax.psum_scatter(partial_input.astype(jnp.bfloat16), 'tp', scatter_dimens...  36.4 us
    another operation x1, loops' own time, shards(): lax.switch(bucket, [partial(attend_slots, slot_count) for slot_count in b...  21.5 us
    cond x21, local copies, waits for them, and re-layouts  17.2 us
    reshape x1, local copies, waits for them, and re-layouts, shards(): pair_grads = lax.psum_scatter(jnp.dot(selector, flat_grads, precision=HIG...  14.5 us
  transfers between devices with their start and end apart: 5, of which 5 were waited for; matrix products, arithmetic and copies ran while one was open for 2% of the time, Pallas kernels for 0%

commit v1 on v0

--- a/solution.py
+++ b/solution.py
@@ -137,9 +137,9 @@
         jnp.bfloat16
     )
     key_value = jnp.concatenate([key_rotated, value_rows], axis=1)
-    gathered = lax.all_gather(key_value, "ctx", axis=0, tiled=True).reshape(
-        block_total, BLOCK, pair_width
-    )
+    gathered = jnp.concatenate(
+        lax.all_to_all(jnp.stack([key_value] * lax.axis_size("ctx")), "ctx", 0, 0), axis=0
+    ).reshape(block_total, BLOCK, pair_width)
     slot_rows = gathered[jnp.clip(path_ids, 0, block_total - 1)]
     query_blocks = queries.reshape(blocks, BLOCK, key_heads, groups, HD)
     upstream_blocks = upstream.reshape(blocks, BLOCK, key_heads, groups, HD)

time: 541 us -> 582 us (1.076)
  waiting for transfers between devices: 352 us -> 397 us
  starting transfers between devices: 0.2 us -> 8.04 us
  local copies, waits for them, and re-layouts: 86.2 us -> 79.2 us
    all_to_all x0 -> x1, waiting for transfers between devices: none -> 96.5 us  [shards(): lax.all_to_all(jnp.stack([key_value] * lax.axis_size('ctx')), 'ctx', 0, 0)]
    all_gather x1 -> x0, waiting for transfers between devices: 54.3 us -> none  [shards(): lax.all_gather(key_value, 'ctx', axis=0, tiled=True)]
    all_to_all x0 -> x1, starting transfers between devices: none -> 7.88 us  [shards(): lax.all_to_all(jnp.stack([key_value] * lax.axis_size('ctx')), 'ctx', 0, 0)]
    another operation x1, local copies, waits for them, and re-layouts: 12 us -> 4.16 us  [shards(): jnp.stack([key_value] * lax.axis_size('ctx'))]
    cond x21 -> x17, local copies, waits for them, and re-layouts: 17.2 us -> 18.4 us
    unnamed x6 -> x5, waiting for transfers between devices: 93.5 us -> 93.4 us
    unnamed x15 -> x17, local copies, waits for them, and re-layouts: 12.4 us -> 12.4 us
where the time goes in v1:
time: 582 us; the launch traced here: 576 us
  waiting for transfers between devices  397 us (68%)
  local copies, waits for them, and re-layouts  79.2 us (14%)
  matrix products  46.5 us (8%)
  loops' own time  21.3 us (4%)
  between operations  14.9 us (3%)
  other arithmetic  9.71 us (2%)
  starting transfers between devices  8.04 us (1%)
    reduce_scatter x1, waiting for transfers between devices, shards(): lax.psum_scatter(jnp.dot(selector, flat_grads, precision=HIGHEST, preferr...  133 us
    all_to_all x1, waiting for transfers between devices, shards(): lax.all_to_all(jnp.stack([key_value] * lax.axis_size('ctx')), 'ctx', 0, 0)  96.5 us
    unnamed x5, waiting for transfers between devices  93.4 us
    all_gather x1, waiting for transfers between devices, shards(): features = lax.all_gather(hidden, 'tp', axis=1, tiled=True)  37.2 us
    reduce_scatter x1, waiting for transfers between devices, shards(): lax.psum_scatter(partial_input.astype(jnp.bfloat16), 'tp', scatter_dimens...  36.5 us
    another operation x1, loops' own time, shards(): lax.switch(bucket, [partial(attend_slots, slot_count) for slot_count in b...  21.3 us
    cond x17, local copies, waits for them, and re-layouts  18.4 us
    reshape x1, local copies, waits for them, and re-layouts, shards(): pair_grads = lax.psum_scatter(jnp.dot(selector, flat_grads, precision=HIG...  14.5 us
  transfers between devices with their start and end apart: 5, of which 5 were waited for; matrix products, arithmetic and copies ran while one was open for 2% of the time, Pallas kernels for 0%

profile of v1, /device:TPU:1, one launch (start us, length us, event | category | flops | bytes accessed | tf_op | source)
XLA Modules:
  0.0 576.2 jit_solution(13633197445151742542)
XLA Ops:
  7.2 0.7 all-gather.2.cloned.1.call-update
  7.9 1.0 convolution_minimum_fusion.3
  8.9 0.2 convolution_minimum_fusion.2
  9.1 0.2 convolution_minimum_fusion.1
  9.2 0.3 fusion.127
  9.7 1.2 broadcast_multiply_fusion
  10.9 37.2 %all-gather.2.cloned.1.call-done = bf16[256,5120]{1,0:T(8,128)(2,1)} async-done(((bf16[256,1280]{1,0:T(8,128)(2,1)}), bf16[256,5120]{1,0:T(8,128)(2,1)}) %all-gather.2.cloned.1.call-update) | async-done | bytes 2621456 | tf_op jit(solution)/shard_map/all_gather | solution.py:127
  48.1 2.6 fusion.129
  50.6 0.1 reshape.514
  50.8 0.5 subtract_convert_fusion.1
  51.3 0.4 pad_maximum_fusion.2
  51.8 3.7 convolution_convert_fusion
  55.5 0.1 copy.271
  55.6 4.2 stack.2
  59.8 7.9 %all-to-all-start = ((bf16[32,256,512]{2,1,0:T(8,128)(2,1)}), bf16[32,256,512]{2,1,0:T(8,128)(2,1)}, u32[]{:S(2)}, u32[]{:S(2)}) async-start(bf16[32,256,512]{2,1,0:T(8,128)(2,1)} %stack.2), calls=%async_computation | async-start | bytes 16777216 | tf_op jit(solution)/shard_map/all_to_all | solution.py:141
  67.7 0.6 reduce_max.36
  69.0 2.2 fusion.108
  71.3 0.6 eq.104
  71.9 96.5 %all-to-all-done = bf16[32,256,512]{2,1,0:T(8,128)(2,1)} async-done(((bf16[32,256,512]{2,1,0:T(8,128)(2,1)}), bf16[32,256,512]{2,1,0:T(8,128)(2,1)}, u32[]{:S(2)}, u32[]{:S(2)}) %all-to-all-start) | async-done | bytes 8388640 | tf_op jit(solution)/shard_map/all_to_all | solution.py:141
  168.4 84.3 %conditional.1 = (f32[16,65536]{1,0:T(8,128)}, bf16[256,1280]{1,0:T(8,128)(2,1)}, bf16[256,1280]{1,0:T(8,128)(2,1)}) conditional(s32[]{:T(128)} %clamp.4, (s32[2]{0:T(128)S(1)}, bf16[32,256,512]{2,1,0:T(8,128)(2,1)}, s32[]{:T(128)}, bf16[256,1280]{1,0:T(8,128)(2,1)S(1)}, bf16[256,1280]{1,0:T(8,128)(2,1)}, ...), branch_computations={%region_4.8_spmd.clone, %region_8.12_spmd.clone, %region_12.16_spm... | conditional | flops 4086446080 | bytes 204010112 | solution.py:172
  175.0 5.4 gather_fusion.1
  180.4 1.3 slice.74
  181.7 1.0 fusion.124
  182.8 2.1 copy.384
  185.0 0.3 and_or_fusion.1
  185.4 2.1 copy.383
  187.4 1.7 reshape.595
  189.1 2.5 reshape.609
  191.7 1.7 copy.363
  193.4 2.5 fusion.30
  196.0 1.1 fusion.26
  197.1 0.3 copy-done.20
  197.4 2.4 multiply_reduce_fusion.1
  199.8 2.6 copy.368
  202.4 2.7 reshape.596
  205.1 4.8 fusion.46
  209.9 4.3 fusion.25
  214.3 0.9 fusion.51
  215.1 0.2 copy-done.11
  215.3 1.1 fusion.52
  216.4 1.9 copy.364
  218.2 3.1 reshape.591
  221.3 3.0 copy.365
  224.3 3.1 reshape.592
  227.4 1.4 copy.369
  228.9 2.6 reshape.597
  231.4 2.1 fusion.29
  233.6 4.5 copy.394
  252.8 12.3 %fusion.115 = f32[64,65536]{1,0:T(8,128)} fusion(f32[16,65536]{1,0:T(8,128)} %get-tuple-element.101, s32[16]{0:T(128)} %eq.104), kind=kOutput, calls=%fused_computation.186 | convolution fusion | flops 805307392 | bytes 20971584 | tf_op jit(solution)/shard_map/dot_general | solution.py:182
  265.0 14.5 %reshape.515 = f32[8192,512]{1,0:T(8,128)} reshape(f32[64,65536]{1,0:T(8,128)} %fusion.115) | data formatting | bytes 33554432 | tf_op jit(solution)/shard_map/reshape | solution.py:184
  279.6 133.1 %reduce-scatter.6.cloned.1.call-done = f32[256,512]{1,0:T(8,128)} async-done(((f32[8192,512]{1,0:T(8,128)}), f32[256,512]{1,0:T(8,128)}) %reduce-scatter.6.cloned.1.call-update) | async-done | bytes 524304 | tf_op jit(solution)/shard_map/reduce_scatter | solution.py:181
  412.7 1.0 slice.81
  413.7 0.1 reshape.516
  413.8 0.5 subtract_convert_fusion
  414.3 0.4 pad_maximum_fusion.3
  414.7 1.0 slice.96
  415.7 7.1 %convolution_bitcast_fusion.3 = f32[5120,512]{0,1:T(8,128)} fusion(bf16[256,5120]{1,0:T(8,128)(2,1)} %all-gather.2.cloned.1.call-done, bf16[256,256]{1,0:T(8,128)(2,1)S(1)} %slice.96, bf16[256,256]{1,0:T(8,128)(2,1)S(1)} %bitcast.334), kind=kOutput, calls=%fused_computation.152 | convolution fusion | flops 1342701568 | bytes 13369344 | tf_op jit(solution)/shard_map/tc,tw->cw/dot_general | solution.py:198
  422.8 11.4 %copy.326 = f32[5120,512]{1,0:T(8,128)} copy(f32[5120,512]{0,1:T(8,128)} %convolution_bitcast_fusion.3) | data formatting | bytes 20971520
  434.3 0.9 fusion.121
  435.3 0.9 copy-done.5
  436.2 2.4 fusion.106
  438.6 92.6 %reduce-scatter.10.cloned.1.call-done = f32[160,512]{1,0:T(8,128)} async-done(((f32[5120,512]{1,0:T(8,128)}), f32[160,512]{1,0:T(8,128)}) %reduce-scatter.10.cloned.1.call-update) | async-done | bytes 327696
  531.3 1.7 fusion.126
  533.0 36.5 %reduce-scatter.8.cloned.1.call-done = bf16[256,1280]{1,0:T(8,128)(2,1)} async-done(((bf16[256,5120]{1,0:T(8,128)(2,1)}), bf16[256,1280]{1,0:T(8,128)(2,1)}) %reduce-scatter.8.cloned.1.call-update) | async-done | bytes 655376 | tf_op jit(solution)/shard_map/reduce_scatter | solution.py:209
  (46 shorter events, 1.0 us)
Async XLA Ops:
  7.2 40.9 %copy-start = (bf16[5120,256]{1,0:T(8,128)(2,1)S(1)}, bf16[5120,256]{1,0:T(8,128)(2,1)}, u32[]{:S(2)}) copy-start(bf16[5120,256]{1,0:T(8,128)(2,1)} %param.11) | copy-start | bytes 7864324
  7.2 40.9 %all-gather.2.cloned.1.call-start = ((), (), s32[]{:S(2)}) async-start(), calls=%async_computation.4 | async-start | bytes 3276800 | tf_op jit(solution)/shard_map/all_gather | solution.py:127
  10.9 44.6 %copy-start.14 = (f32[2,128,64]{2,1,0:T(8,128)}, f32[2,128,64]{2,1,0:T(8,128)S(1)}, u32[]{:S(2)}) copy-start(f32[2,128,64]{2,1,0:T(8,128)S(1)} %get-tuple-element.288) | copy-start | bytes 196612
  59.8 108.6 %copy-start.8 = (bf16[256,1280]{1,0:T(8,128)(2,1)S(1)}, bf16[256,1280]{1,0:T(8,128)(2,1)}, u32[]{:S(2)}) copy-start(bf16[256,1280]{1,0:T(8,128)(2,1)} %param.10) | copy-start | bytes 1966084
  59.8 108.6 %all-to-all-start = ((bf16[32,256,512]{2,1,0:T(8,128)(2,1)}), bf16[32,256,512]{2,1,0:T(8,128)(2,1)}, u32[]{:S(2)}, u32[]{:S(2)}) async-start(bf16[32,256,512]{2,1,0:T(8,128)(2,1)} %stack.2), calls=%async_computation | async-start | bytes 16777216 | tf_op jit(solution)/shard_map/all_to_all | solution.py:141
  67.7 345.0 %reduce-scatter.6.cloned.1.call-start = ((), (), s32[]{:S(2)}) async-start(), calls=%async_computation.5 | async-start | bytes 17301504 | tf_op jit(solution)/shard_map/reduce_scatter | solution.py:181
  195.9 3.9 copy-start.4
  196.0 1.4 copy-start.20
  205.1 4.8 copy-start.21
  209.9 4.3 copy-start.12
  214.2 1.0 copy-start.11
  279.5 134.3 %copy-start.15 = (f32[2,128,64]{2,1,0:T(8,128)S(1)}, f32[2,128,64]{2,1,0:T(8,128)}, u32[]{:S(2)}) copy-start(f32[2,128,64]{2,1,0:T(8,128)} %copy-done.14) | copy-start | bytes 196612
  279.5 134.3 %copy-start.22 = (f32[2,128,64]{2,1,0:T(8,128)S(1)}, f32[2,128,64]{2,1,0:T(8,128)}, u32[]{:S(2)}) copy-start(f32[2,128,64]{2,1,0:T(8,128)} %get-tuple-element.286) | copy-start | bytes 196612
  279.6 251.7 %reduce-scatter.10.cloned.1.call-start = ((), (), s32[]{:S(2)}) async-start(), calls=%async_computation.7 | async-start | bytes 10813440
  434.2 1.0 copy-start.19
  434.2 135.2 %reduce-scatter.8.cloned.1.call-start = ((), (), s32[]{:S(2)}) async-start(), calls=%async_computation.6 | async-start | bytes 3276800 | tf_op jit(solution)/shard_map/reduce_scatter | solution.py:209
  434.3 1.9 copy-start.5
Sparse Core Ops, SparseCore 0:
  9.6 38.3 all-gather.1
  279.7 132.9 reduce-scatter.5
  434.4 96.8 reduce-scatter.9
  534.1 35.3 reduce-scatter.7
